TPU v7x, 768 devices: a whole 4x8x12 slice. The times are simulated.
768 devices in a mesh: section: 8 (over x, y_lo), seq: 24 (over z, core), rep: 4 (over y_hi).
Axes of the slice: x: 4, y: 8 (y_hi: 4, y_lo: 2; y = y_hi * 2 + y_lo), z: 12, core: 2. Of those that a mesh axis runs over, the one named last changes fastest.
Arguments:
- char_queries: bfloat16 [4, 8, 6144, 2048], P('rep', 'section', 'seq'), may hold values from -34 to 34
- char_keys: bfloat16 [4, 8, 6144, 2048], P('rep', 'section', 'seq'), may hold values from -6 to 6
- char_values: bfloat16 [4, 8, 6144, 2048], P('rep', 'section', 'seq'), may hold values from -48 to 48
- doc_starts: int32 [4, 8, 48], P('rep', 'section'), may hold values from 0 to 6143, as said below
- key_weight: bfloat16 [8, 2048, 1024], P('section'), may hold values from -0.125 to 0.125
- norm_gain: float32 [8, 2048], P('section'), may hold values from 0.25 to 1.75
- stashed: bfloat16 [4, 8, 2, 1536, 2048], P('rep', 'section', None, 'seq'), may hold values from -48 to 48
- cotangent: bfloat16 [4, 8, 1536, 1024], P('rep', 'section', 'seq'), may hold values from -6 to 6
- plan_slot: int32 [4, 8], P('rep', 'section'), may hold values from 0 to 1
Outputs:
- mol_keys: bfloat16 [4, 8, 1536, 1024], P('rep', 'section', 'seq')
- upstream_grad: bfloat16 [4, 8, 1536, 2048], P('rep', 'section', 'seq')
- gain_update: float32 [8, 2048], P('section')
Inputs may be any that keep to these rules, and one draw needn't show every extreme that they name: `doc_starts`: each row of offsets rises strictly, begins with 0 and ends with 6143.
All inputs are finite; a program needn't handle non-finite values.
Results may differ from a plain program's by a relative error of at most 0.012.
Values may be sent and summed in bfloat16 or wider, within the bound.
A program may use at most 64 MiB of HBM per device.

v0:
```python
import math

import jax
import jax.numpy as jnp
from jax import lax
from jax.sharding import PartitionSpec as P

HEADS = 32
HEAD_DIM = 64
POOL = 4
WINDOW = 128


EPS_NORM = 1e-05
EPS_STEP = 1e-06


def from_behind(value, axis, steps):
    count = lax.axis_size(axis)
    first, last = (max(0, -steps), min(count, count - steps))
    return lax.ppermute(value, axis, [(source, source + steps) for source in range(first, last)])


def passed_along(block, axis, distance):
    devices = range(lax.axis_size(axis))
    route = [((i - distance) % len(devices), i) for i in devices]
    return lax.ppermute(block, axis, route)


def doc_index(positions, offsets):
    return jnp.sum((offsets[None, :] <= positions[:, None]).astype(jnp.int32), axis=1)


def attend(queries, keys_all, values_all, query_pos, key_pos, offsets):
    row_count = queries.shape[0]
    key_count = keys_all.shape[0]
    width = queries.shape[1]
    query_doc = doc_index(query_pos, offsets)
    key_doc = doc_index(key_pos, offsets)
    allowed = (
        (key_doc[None, :] == query_doc[:, None])
        & (key_pos[None, :] <= query_pos[:, None])
        & (key_pos[None, :] > query_pos[:, None] - WINDOW)
    )
    head_group = min(HEADS, 8)
    group_count = HEADS // head_group
    group_width = head_group * HEAD_DIM

    def one_group(group_index):
        group_start = group_index * group_width
        group_queries = lax.dynamic_slice_in_dim(queries, group_start, group_width, 1).reshape(
            row_count, head_group, HEAD_DIM
        )
        group_keys = lax.dynamic_slice_in_dim(keys_all, group_start, group_width, 1).reshape(
            key_count, head_group, HEAD_DIM
        )
        group_values = lax.dynamic_slice_in_dim(values_all, group_start, group_width, 1).reshape(
            key_count, head_group, HEAD_DIM
        )
        scores = jnp.einsum(
            "qhd,khd->hqk", group_queries, group_keys, preferred_element_type=jnp.float32
        ) * (1.0 / math.sqrt(HEAD_DIM))
        scores = jnp.where(allowed[None, :, :], scores, -1e30)
        row_max = jnp.max(scores, axis=2, keepdims=True)
        weights = jnp.exp(scores - row_max)
        row_total = jnp.sum(weights, axis=2, keepdims=True)
        rounded = weights.astype(jnp.bfloat16)
        mixed_heads = jnp.einsum(
            "hqk,khd->qhd", rounded, group_values, preferred_element_type=jnp.float32
        )
        return (
            (mixed_heads / jnp.transpose(row_total, (1, 0, 2)))
            .reshape(row_count, group_width)
            .astype(jnp.bfloat16)
        )

    groups = lax.map(one_group, jnp.arange(group_count, dtype=jnp.int32))
    return jnp.transpose(groups, (1, 0, 2)).reshape(row_count, width)


def shorten(rows_in):
    return jnp.mean(rows_in.astype(jnp.float32).reshape(-1, POOL, rows_in.shape[1]), axis=1).astype(
        jnp.bfloat16
    )


def local(
    char_queries,
    char_keys,
    char_values,
    doc_starts,
    key_weight,
    norm_gain,
    stashed,
    cotangent,
    plan_slot,
):
    queries = char_queries[0, 0]
    own_keys = char_keys[0, 0]
    own_values = char_values[0, 0]
    offsets = doc_starts[0, 0]
    row_count = queries.shape[0]
    first_pos = lax.axis_index("seq") * row_count
    query_pos = first_pos + jnp.arange(row_count, dtype=jnp.int32)
    far_keys, far_values = from_behind((own_keys, own_values), "seq", 1)
    far_pos = first_pos - row_count + jnp.arange(row_count, dtype=jnp.int32)
    keys_all = jnp.concatenate([far_keys, own_keys], axis=0)
    values_all = jnp.concatenate([far_values, own_values], axis=0)
    key_pos = jnp.concatenate([far_pos, query_pos], axis=0)
    attended = attend(queries, keys_all, values_all, query_pos, key_pos, offsets)
    arrived = shorten(passed_along(attended, "section", 1))
    projection = key_weight[0]
    gain_row = norm_gain[0]
    as_float = arrived.astype(jnp.float32)
    inv_norm = lax.rsqrt(jnp.mean(as_float * as_float, axis=1, keepdims=True) + EPS_NORM)
    normed = (as_float * inv_norm * gain_row).astype(jnp.bfloat16)
    mol_rows = jnp.dot(normed, projection, preferred_element_type=jnp.float32).astype(jnp.bfloat16)
    held_rows = lax.dynamic_index_in_dim(stashed[0, 0], plan_slot[0, 0], 0, keepdims=False).astype(
        jnp.float32
    )
    back_grad = lax.dot_general(
        cotangent[0, 0], projection, (((1,), (1,)), ((), ())), preferred_element_type=jnp.float32
    )
    inv_rms = lax.rsqrt(jnp.mean(held_rows * held_rows, axis=1, keepdims=True) + EPS_NORM)
    whitened = held_rows * inv_rms
    gain_term = jnp.sum(back_grad * whitened, axis=0)
    summed = lax.psum(gain_term, ("seq", "rep"))
    update = summed / jnp.sqrt(jnp.mean(summed * summed) + EPS_STEP)
    scaled = back_grad * gain_row
    dinput = (
        inv_rms * (scaled - whitened * jnp.mean(scaled * whitened, axis=1, keepdims=True))
    ).astype(jnp.bfloat16)
    upstream = passed_along(dinput, "section", -1)
    return (mol_rows[None, None], upstream[None, None], update[None])


def solution(mesh):
    in_specs = (
        P("rep", "section", "seq", None),
        P("rep", "section", "seq", None),
        P("rep", "section", "seq", None),
        P("rep", "section", None),
        P("section", None, None),
        P("section", None),
        P("rep", "section", None, "seq", None),
        P("rep", "section", "seq", None),
        P("rep", "section"),
    )
    out_specs = (
        P("rep", "section", "seq", None),
        P("rep", "section", "seq", None),
        P("section", None),
    )
    return jax.shard_map(local, mesh=mesh, in_specs=in_specs, out_specs=out_specs, check_vma=False)
```

profile of v0, /device:TPU:266, one launch (start us, length us, event | category | flops | bytes accessed | tf_op | source)
XLA Modules:
  0.0 311.6 jit_solution(10957706774075382755)
XLA Ops:
  0.7 1.5 copy.19
  2.2 1.9 collective-permute-start
  4.2 2.3 copy.21
  6.4 4.4 %collective-permute-start.1 = (bf16[256,2048]{0,1:T(8,128)(2,1)}, bf16[256,2048]{0,1:T(8,128)(2,1)}, u32[]{:S(2)}, u32[]{:S(2)}) collective-permute-start(bf16[256,2048]{0,1:T(8,128)(2,1)} %bitcast.2), channel_id=1, source_target_pairs={{0,4},{4,8},{8,12},{12,16},{16,20},{20,24},{24,28},{28,32},{32,36}... | collective-permute-start | bytes 3145736 | tf_op jit(solution)/shard_map/ppermute | solution.py:21
  10.8 1.5 copy.20
  13.4 6.3 %collective-permute-done = bf16[256,2048]{0,1:T(8,128)(2,1)} collective-permute-done((bf16[256,2048]{0,1:T(8,128)(2,1)S(1)}, bf16[256,2048]{0,1:T(8,128)(2,1)}, u32[]{:S(2)}, u32[]{:S(2)}) %collective-permute-start) | collective-permute-done | bytes 1048608 | tf_op jit(solution)/shard_map/ppermute | solution.py:21
  19.7 1.7 pad_maximum_fusion
  21.4 9.5 %collective-permute-done.1 = bf16[256,2048]{0,1:T(8,128)(2,1)} collective-permute-done((bf16[256,2048]{0,1:T(8,128)(2,1)}, bf16[256,2048]{0,1:T(8,128)(2,1)}, u32[]{:S(2)}, u32[]{:S(2)}) %collective-permute-start.1) | collective-permute-done | bytes 1048608 | tf_op jit(solution)/shard_map/ppermute | solution.py:21
  30.9 3.0 pad_maximum_fusion.1
  33.9 27.2 %while.11 = (s32[]{:T(128)}, bf16[4,256,512]{1,2,0:T(8,128)(2,1)}, s32[4]{0:T(128)S(1)}, bf16[512,2048]{0,1:T(8,128)(2,1)S(1)}, bf16[256,2048]{0,1:T(8,128)(2,1)...) while((s32[]{:T(128)}, bf16[4,256,512]{1,2,0:T(8,128)(2,1)}, ...), condition=%wide.region_5.6_spmd.clone, body=%wide.region_2.5_spmd.clone.sunk | while | flops 280883200 | bytes 17874140 | solution.py:77
  33.9 0.6 dynamic_slice.34
  35.2 1.1 constant_dynamic-slice_fusion.5
  36.3 0.2 compare_and_fusion.2
  36.6 0.9 fusion.60
  37.5 1.3 fusion.61
  38.8 1.2 fusion.62
  40.0 0.7 constant_dynamic-update-slice_fusion.2
  40.8 0.6 dynamic_slice.34
  42.0 1.1 constant_dynamic-slice_fusion.5
  43.1 0.2 compare_and_fusion.2
  43.4 0.9 fusion.60
  44.3 1.3 fusion.61
  45.6 1.2 fusion.62
  46.8 0.7 constant_dynamic-update-slice_fusion.2
  47.5 0.6 dynamic_slice.34
  48.8 1.1 constant_dynamic-slice_fusion.5
  49.9 0.2 compare_and_fusion.2
  50.1 0.9 fusion.60
  51.1 1.3 fusion.61
  52.4 1.2 fusion.62
  53.6 0.7 constant_dynamic-update-slice_fusion.2
  54.3 0.6 dynamic_slice.34
  55.6 1.1 constant_dynamic-slice_fusion.5
  56.9 0.9 fusion.60
  57.9 1.3 fusion.61
  59.2 1.2 fusion.62
  60.4 0.7 constant_dynamic-update-slice_fusion.2
  61.1 1.5 copy.22
  62.7 3.3 %collective-permute-start.2 = (bf16[256,2048]{1,0:T(8,128)(2,1)S(1)}, bf16[256,2048]{1,0:T(8,128)(2,1)}, u32[]{:S(2)}, u32[]{:S(2)}) collective-permute-start(bf16[256,2048]{1,0:T(8,128)(2,1)S(1)} %copy.22), channel_id=1, source_target_pairs={{672,0},{0,96},{96,192},{192,288},{288,384},{384,480},{480,576},{5... | collective-permute-start | bytes 3145736 | tf_op jit(solution)/shard_map/ppermute | solution.py:27
  66.0 3.7 %fusion.39 = (f32[2048]{0:T(1024)S(1)}, f32[64]{0:T(128)S(1)}, f32[64,2048]{1,0:T(8,128)S(1)}) fusion(f32[64]{0:T(128)S(1)} %add_rsqrt_fusion, bf16[1,1,2,64,2048]{4,3,2,1,0:T(8,128)(2,1)} %param.17, s32[]{:T(128)S(6)} %select_n.13, f32[2048]{0:T(1024)S(1)} %bitcast.87, bf16[1,2048,1024]{2,1,0:T(8,128)(2,1)} %param.15, bf16[1,1,64,1024]{3,2,1,0:T(8,128)(2,1)S(1)} %copy-done), kind=kOutput, calls=%fused_computation.40 | convolution fusion | flops 269350848 | bytes 5128708 | tf_op jit(solution)/shard_map/dot_general | solution.py:121
  69.9 2.6 collective-permute-start.3
  72.5 229.5 %psum.7 = f32[2048]{0:T(1024)S(1)} all-reduce(f32[2048]{0:T(1024)S(1)} %get-tuple-element.70), channel_id=1, replica_groups=mesh['section'=8,'seq'=24,'rep'=4] {'seq','rep'}, use_global_device_ids=true, to_apply=%region_11.12 | all-reduce | flops 2048 | bytes 16384 | tf_op jit(solution)/shard_map/psum | solution.py:127
  302.0 0.6 multiply_reduce_fusion
  303.3 0.6 broadcast_divide_fusion
  303.9 1.7 reshape.81
  305.6 1.3 reduce_sum.83
  307.1 3.7 %fusion.26 = bf16[1,1,64,1024]{3,2,1,0:T(8,128)(2,1)} fusion(bf16[1,2048,1024]{2,1,0:T(8,128)(2,1)} %param.15, f32[2048]{0:T(1024)S(1)} %bitcast.89, f32[64]{0:T(128)S(1)} %add_rsqrt_fusion.1, f32[64,2048]{1,0:T(8,128)S(1)} %reduce_sum.83), kind=kOutput, calls=%fused_computation.25 | convolution fusion | flops 269287424 | bytes 4858112 | tf_op jit(solution)/shard_map/dot_general | solution.py:117
  310.9 0.7 copy.32
  (32 shorter events, 1.1 us)
Async XLA Ops:
  0.6 65.3 %copy-start = (bf16[1,1,64,1024]{3,2,1,0:T(8,128)(2,1)S(1)}, bf16[1,1,64,1024]{3,2,1,0:T(8,128)(2,1)}, u32[]{:S(2)}) copy-start(bf16[1,1,64,1024]{3,2,1,0:T(8,128)(2,1)} %param.18) | copy-start | bytes 393220
  0.6 12.3 %copy-start.2 = (bf16[1,1,2,64,2048]{4,3,2,1,0:T(8,128)(2,1)S(1)}, bf16[1,1,2,64,2048]{4,3,2,1,0:T(8,128)(2,1)}, u32[]{:S(2)}) copy-start(bf16[1,1,2,64,2048]{4,3,2,1,0:T(8,128)(2,1)} %param.17) | copy-start | bytes 1572868
  0.7 12.5 %copy-start.5 = (s32[1,1,48]{2,1,0:T(1,128)S(1)}, s32[1,1,48]{2,1,0:T(1,128)}, u32[]{:S(2)}) copy-start(s32[1,1,48]{2,1,0:T(1,128)} %param.14) | copy-start | bytes 580
  2.2 11.2 %copy-start.1 = (bf16[1,1,256,2048]{2,3,1,0:T(8,128)(2,1)}, bf16[1,1,256,2048]{2,3,1,0:T(8,128)(2,1)S(1)}, u32[]{:S(2)}) copy-start(bf16[1,1,256,2048]{2,3,1,0:T(8,128)(2,1)S(1)} %copy.19) | copy-start | bytes 3145732
  2.2 17.4 %collective-permute-start = (bf16[256,2048]{0,1:T(8,128)(2,1)S(1)}, bf16[256,2048]{0,1:T(8,128)(2,1)}, u32[]{:S(2)}, u32[]{:S(2)}) collective-permute-start(bf16[256,2048]{0,1:T(8,128)(2,1)S(1)} %bitcast.82), channel_id=1, source_target_pairs={{0,4},{4,8},{8,12},{12,16},{16,20},{20,24},{24,28},{28,32},{32,36}... | collective-permute-start | bytes 3145736 | tf_op jit(solution)/shard_map/ppermute | solution.py:21
  6.4 24.5 %collective-permute-start.1 = (bf16[256,2048]{0,1:T(8,128)(2,1)}, bf16[256,2048]{0,1:T(8,128)(2,1)}, u32[]{:S(2)}, u32[]{:S(2)}) collective-permute-start(bf16[256,2048]{0,1:T(8,128)(2,1)} %bitcast.2), channel_id=1, source_target_pairs={{0,4},{4,8},{8,12},{12,16},{16,20},{20,24},{24,28},{28,32},{32,36}... | collective-permute-start | bytes 3145736 | tf_op jit(solution)/shard_map/ppermute | solution.py:21
  33.9 32.0 %copy-start.4 = (f32[1,2048]{1,0:T(1,128)S(1)}, f32[1,2048]{1,0:T(1,128)}, u32[]{:S(2)}) copy-start(f32[1,2048]{1,0:T(1,128)} %param.16) | copy-start | bytes 24580
  61.1 8.6 %copy-start.3 = (bf16[1,1,2,64,2048]{4,3,2,1,0:T(8,128)(2,1)S(1)}, bf16[1,1,2,64,2048]{4,3,2,1,0:T(8,128)(2,1)}, u32[]{:S(2)}) copy-start(bf16[1,1,2,64,2048]{4,3,2,1,0:T(8,128)(2,1)} %param.17) | copy-start | bytes 1572868
  62.7 241.2 %collective-permute-start.2 = (bf16[256,2048]{1,0:T(8,128)(2,1)S(1)}, bf16[256,2048]{1,0:T(8,128)(2,1)}, u32[]{:S(2)}, u32[]{:S(2)}) collective-permute-start(bf16[256,2048]{1,0:T(8,128)(2,1)S(1)} %copy.22), channel_id=1, source_target_pairs={{672,0},{0,96},{96,192},{192,288},{288,384},{384,480},{480,576},{5... | collective-permute-start | bytes 3145736 | tf_op jit(solution)/shard_map/ppermute | solution.py:27
  69.9 233.9 %collective-permute-start.3 = (bf16[64,2048]{1,0:T(8,128)(2,1)S(1)}, bf16[64,2048]{1,0:T(8,128)(2,1)S(1)}, u32[]{:S(2)}, u32[]{:S(2)}) collective-permute-start(bf16[64,2048]{1,0:T(8,128)(2,1)S(1)} %fusion.38), channel_id=1, source_target_pairs={{96,0},{192,96},{288,192},{384,288},{480,384},{576,480},{672,576},... | collective-permute-start | bytes 786440 | tf_op jit(solution)/shard_map/ppermute | solution.py:27
where the time goes:
time: 312 us
  blocking collectives  229 us (73%)
  local copies, waits for them, and re-layouts  19.1 us (6%)
  matrix products  16.1 us (5%)
  waiting for transfers between devices  15.8 us (5%)
  other arithmetic  14 us (4%)
  starting transfers between devices  12.1 us (4%)
    psum x1, blocking collectives, local(): summed = lax.psum(gain_term, ('seq', 'rep'))  229 us
    ppermute x2, waiting for transfers between devices, from_behind(): lax.ppermute(value, axis, [(source, source + steps) for source in range(f...  15.8 us
    ppermute x2, starting transfers between devices, from_behind(): lax.ppermute(value, axis, [(source, source + steps) for source in range(f...  6.29 us
  transfers between devices with their start and end apart: 4, of which 2 were waited for; matrix products, arithmetic and copies ran while one was open for 4% of the time, Pallas kernels for 0%

commit v1 on v0

v1 whole, which is shorter than its diff:
```python
import functools
import math

import jax
import jax.numpy as jnp
from jax import lax
from jax.experimental import pallas as pl
from jax.experimental.pallas import tpu as pltpu
from jax.sharding import PartitionSpec as P

HEAD_DIM = 64
POOL = 4
WINDOW = 128
EPS_NORM = 1e-05
EPS_STEP = 1e-06
LOG2E = math.log2(math.e)
MESH = pl.DeviceIdType.MESH
F32 = jnp.float32
BF16 = jnp.bfloat16


def kernel(
    nsec,
    nseq,
    nrep,
    chunks,
    q_hbm,
    k_hbm,
    v_hbm,
    doc_ref,
    w_hbm,
    gain_ref,
    st_hbm,
    cot_hbm,
    slot_ref,
    mol_ref,
    up_ref,
    gu_ref,
    q_raw,
    q_buf,
    k_buf,
    v_buf,
    w_buf,
    st_buf,
    cot_buf,
    bias,
    bg_buf,
    din,
    pooled,
    arrived,
    acc,
    g_own,
    r1,
    r2,
    r3,
    loc_sem,
    kv_send,
    kv_recv,
    up_send,
    up_recv,
    po_send,
    po_recv,
    p1_send,
    p1_recv,
    p2_send,
    p2_recv,
    p3_send,
    p3_recv,
):
    rows, width = q_raw.shape
    half = rows // 2
    mol_rows, key_width = acc.shape
    mol_half = mol_rows // 2
    nz = nseq // 2
    nown = nrep * 2
    part = width // nown
    cw = width // chunks
    pairs = cw // 128

    sec = lax.axis_index("section")
    seq = lax.axis_index("seq")
    rep = lax.axis_index("rep")
    core = lax.rem(seq, 2)
    z = lax.div(seq, 2)
    me = rep * 2 + core
    sec_next = lax.rem(sec + 1, nsec)
    sec_prev = lax.rem(sec + nsec - 1, nsec)
    seq_next = lax.rem(seq + 1, nseq)
    seq_prev = lax.rem(seq + nseq - 1, nseq)
    across = lax.rem(seq + nseq + 2 * core - 1, nseq)

    def owner_id(d):
        other = lax.rem(me + d, nown)
        return other, {"seq": z * 2 + lax.rem(other, 2), "rep": lax.div(other, 2)}

    def z_id(d):
        other = lax.rem(z + d, nz)
        return other, {"seq": other * 2 + core}

    loads = {}

    def load(name, index, src, dst):
        loads[name] = pltpu.make_async_copy(src, dst, loc_sem.at[index])
        loads[name].start()

    load("cot", 0, cot_hbm.at[0, 0], cot_buf)
    load("st", 1, st_hbm.at[0, 0], st_buf)
    load("w", 2, w_hbm.at[0], w_buf)
    load("q", 3, q_hbm.at[0, 0], q_raw)
    load("k", 4, k_hbm.at[0, 0], k_buf.at[pl.ds(half, rows)])
    load("v", 5, v_hbm.at[0, 0], v_buf.at[pl.ds(half, rows)])

    barrier = pltpu.get_barrier_semaphore()
    peers = [{"seq": across}, {"section": sec_next}, {"section": sec_prev}]
    peers += [owner_id(d)[1] for d in range(1, nown)]
    peers += [z_id(d)[1] for d in range(1, nz)]
    for peer in peers:
        pl.semaphore_signal(barrier, inc=1, device_id=peer, device_id_type=MESH)
    pl.semaphore_wait(barrier, len(peers))

    def remote(src, dst, send, recv, to):
        return pltpu.make_async_remote_copy(
            src_ref=src, dst_ref=dst, send_sem=send, recv_sem=recv, device_id=to, device_id_type=MESH
        )

    halo = []
    for c in range(chunks):
        cols = pl.ds(c * cw, cw)
        for i, (src, dst) in enumerate(((k_hbm, k_buf), (v_hbm, v_buf))):
            copy = remote(
                src.at[0, 0, pl.ds(half, half), cols],
                dst.at[pl.ds(0, half), cols],
                kv_send.at[2 * c + i],
                kv_recv.at[2 * c + i],
                {"seq": seq_next},
            )
            copy.start()
            halo.append(copy)

    for name in ("cot", "st", "w"):
        loads[name].wait()
    slot = slot_ref[0, 0]
    square = jnp.zeros((mol_rows, 1), F32)
    for c in range(chunks):
        cols = pl.ds(c * cw, cw)
        held = st_buf[slot, :, cols].astype(F32)
        square += jnp.sum(held * held, axis=1, keepdims=True)
    inv_rms = lax.rsqrt(square / width + EPS_NORM)
    cot = cot_buf[...]
    mixed = jnp.zeros((mol_rows, 1), F32)
    for c in range(chunks):
        cols = pl.ds(c * cw, cw)
        back = lax.dot_general(cot, w_buf[cols, :], (((1,), (1,)), ((), ())), preferred_element_type=F32)
        whitened = st_buf[slot, :, cols].astype(F32) * inv_rms
        term = back * whitened
        scaled = back * gain_ref[:, cols]
        bg_buf[:, cols] = scaled
        mixed += jnp.sum(scaled * whitened, axis=1, keepdims=True)
        total = jnp.sum(term, axis=0, keepdims=True)
        for i in range(cw // part):
            g_own[c * (cw // part) + i] = total[:, i * part : (i + 1) * part]
    mixed = mixed / width
    for c in range(chunks):
        cols = pl.ds(c * cw, cw)
        whitened = st_buf[slot, :, cols].astype(F32) * inv_rms
        din[:, cols] = (inv_rms * (bg_buf[:, cols] - whitened * mixed)).astype(BF16)

    phase1 = []
    for d in range(1, nown):
        other, to = owner_id(d)
        copy = remote(g_own.at[other], r1.at[d], p1_send.at[d], p1_recv.at[d], to)
        copy.start()
        phase1.append(copy)
    up_copy = remote(din, up_ref.at[0, 0], up_send.at[0], up_recv.at[0], {"section": sec_prev})
    up_copy.start()

    loads["q"].wait()
    row = lax.broadcasted_iota(jnp.int32, (rows, rows), 0)
    col = lax.broadcasted_iota(jnp.int32, (rows, rows), 1)
    inner = lax.rem(row, half)
    source = (row - inner) + POOL * lax.rem(inner, mol_half) + lax.div(inner, mol_half)
    perm = jnp.where(col == source, F32(1.0 / math.sqrt(HEAD_DIM)), F32(0.0)).astype(BF16)
    lane = lax.rem(lax.broadcasted_iota(jnp.int32, (rows, 128), 1), 128)
    for c in range(chunks):
        moved = jnp.dot(perm, q_raw[:, pl.ds(c * cw, cw)], preferred_element_type=F32)
        for i in range(pairs):
            cols = pl.ds(c * cw + i * 128, 128)
            piece = moved[:, i * 128 : (i + 1) * 128]
            first = jnp.where(lane < HEAD_DIM, piece, 0.0).astype(BF16)
            second = jnp.where(lane < HEAD_DIM, 0.0, piece).astype(BF16)
            for b in range(2):
                q_buf[b, pl.ds(0, half), cols] = first[b * half : (b + 1) * half]
                q_buf[b, pl.ds(half, half), cols] = second[b * half : (b + 1) * half]

    offsets = doc_ref[0].astype(F32)
    q_row = lax.broadcasted_iota(jnp.int32, (half, 1), 0)
    q_in = POOL * lax.rem(q_row, mol_half) + lax.div(q_row, mol_half)
    k_in = lax.broadcasted_iota(jnp.int32, (half, 2 * half), 1)
    for b in range(2):
        start = seq * rows + b * half
        q_pos = (q_in + start).astype(F32)
        begin = jnp.max(jnp.where(offsets <= q_pos, offsets, -1.0), axis=1, keepdims=True)
        allowed = (
            (k_in > q_in + (half - WINDOW)) & (k_in <= q_in + half) & ((k_in + (start - half)).astype(F32) >= begin)
        )
        bias[b] = jnp.where(allowed, F32(0.0), F32(-1e30))

    lane_o = lax.broadcasted_iota(jnp.int32, (half, 128), 1)
    fours = jnp.full((2 * half, 128), POOL, BF16)

    def attend(b, first_pair, count):
        def one_pair(i, carry):
            cols = pl.ds(pl.multiple_of((first_pair + i) * 128, 128), 128)
            keys = k_buf[pl.ds(b * half, 2 * half), cols]
            values = v_buf[pl.ds(b * half, 2 * half), cols]
            scores = lax.dot_general(q_buf[b, :, cols], keys, (((1,), (1,)), ((), ())), preferred_element_type=F32)
            blocked = bias[b]
            weights = []
            for h in range(2):
                s = scores[h * half : (h + 1) * half] + blocked
                top = jnp.max(s, axis=1, keepdims=True)
                weights.append(jnp.exp2((s - top) * LOG2E).astype(BF16))
            mixed_heads = jnp.dot(
                jnp.concatenate(weights, axis=0),
                jnp.concatenate([values, fours], axis=1),
                preferred_element_type=F32,
            )
            low = lane_o < HEAD_DIM
            top_half, bottom_half = mixed_heads[:half], mixed_heads[half:]
            out = jnp.where(low, top_half[:, :128], bottom_half[:, :128]) / jnp.where(
                low, top_half[:, 128:], bottom_half[:, 128:]
            )
            mean = out[:mol_half]
            for t in range(1, POOL):
                mean += out[t * mol_half : (t + 1) * mol_half]
            pooled[pl.ds(b * mol_half, mol_half), cols] = mean.astype(BF16)
            return carry

        lax.fori_loop(0, count, one_pair, 0)

    relay = []

    def send_pooled(index, rows_at, cols):
        copy = remote(
            pooled.at[rows_at, cols],
            arrived.at[rows_at, cols],
            po_send.at[index],
            po_recv.at[index],
            {"section": sec_next},
        )
        copy.start()
        relay.append(copy)

    loads["k"].wait()
    loads["v"].wait()
    attend(1, 0, width // 128)
    send_pooled(chunks, pl.ds(mol_half, mol_half), pl.ds(0, width))

    for copy in phase1:
        copy.wait_recv()
    summed = g_own[me]
    for d in range(1, nown):
        summed += r1[d]
    r2[z] = summed
    phase2 = []
    for d in range(1, nz):
        other, to = z_id(d)
        copy = remote(r2.at[z], r2.at[z], p2_send.at[d], p2_recv.at[d], to)
        copy.start()
        phase2.append(copy)

    acc[...] = jnp.zeros_like(acc)
    square = jnp.zeros((mol_rows, 1), F32)
    phase3 = []

    def project(c, square):
        cols = pl.ds(c * cw, cw)
        relay[1 + c].wait_recv()
        got = arrived[:, cols].astype(F32)
        acc[...] += jnp.dot((got * gain_ref[:, cols]).astype(BF16), w_buf[cols, :], preferred_element_type=F32)
        return square + jnp.sum(got * got, axis=1, keepdims=True)

    for c in range(chunks):
        halo[2 * c].wait_recv()
        halo[2 * c + 1].wait_recv()
        attend(0, c * pairs, pairs)
        send_pooled(c, pl.ds(0, mol_half), pl.ds(c * cw, cw))
        if c == 0:
            relay[0].wait_recv()
        else:
            square = project(c - 1, square)
        if c == chunks - 2:
            for d in range(1, nz):
                other = lax.rem(z + nz - d, nz)
                remote(r2.at[z], r2.at[other], p2_send.at[d], p2_recv.at[d], {"seq": seq_next}).wait_recv()
            summed = r2[0]
            for i in range(1, nz):
                summed += r2[i]
            r3[me] = summed
            for d in range(1, nown):
                other, to = owner_id(d)
                copy = remote(r3.at[me], r3.at[me], p3_send.at[d], p3_recv.at[d], to)
                copy.start()
                phase3.append(copy)

    for d in range(1, nown):
        other = lax.rem(me + nown - d, nown)
        remote(r3.at[me], r3.at[other], p3_send.at[d], p3_recv.at[d], {"seq": seq_next}).wait_recv()
    power = jnp.zeros((1, 1), F32)
    for i in range(nown):
        power += jnp.sum(r3[i] * r3[i], axis=1, keepdims=True)
    inv_step = 1.0 / jnp.sqrt(power / width + EPS_STEP)
    for i in range(nown):
        gu_ref[:, pl.ds(i * part, part)] = r3[i] * inv_step

    for copy in halo:
        copy.wait_send()
    for copy in (*phase1, *phase2, *phase3):
        copy.wait_send()
    up_copy.wait()

    square = project(chunks - 1, square)
    mol_ref[0, 0] = (acc[...] * lax.rsqrt(square / width + EPS_NORM)).astype(BF16)
    for copy in relay:
        copy.wait_send()


def solution(mesh):
    nsec, nseq, nrep = (mesh.shape[a] for a in ("section", "seq", "rep"))

    def local(q, k, v, doc_starts, w, gain, stashed, cotangent, plan_slot):
        rows, width = q.shape[2:]
        key_width = w.shape[2]
        slots, mol_rows = stashed.shape[2:4]
        half = rows // 2
        chunks = 4 if width >= 2048 else 2
        nz, nown = nseq // 2, nrep * 2
        part = width // nown
        hbm = pl.BlockSpec(memory_space=pl.ANY)
        vmem = pl.BlockSpec(memory_space=pltpu.VMEM)
        smem = pl.BlockSpec(memory_space=pltpu.SMEM)
        dma = pltpu.SemaphoreType.DMA
        return pl.pallas_call(
            functools.partial(kernel, nsec, nseq, nrep, chunks),
            out_shape=(
                jax.ShapeDtypeStruct((1, 1, mol_rows, key_width), BF16),
                jax.ShapeDtypeStruct((1, 1, mol_rows, width), BF16),
                jax.ShapeDtypeStruct((1, width), F32),
            ),
            in_specs=[hbm, hbm, hbm, vmem, hbm, vmem, hbm, hbm, smem],
            out_specs=(vmem, hbm, vmem),
            scratch_shapes=[
                pltpu.VMEM((rows, width), BF16),
                pltpu.VMEM((2, rows, width), BF16),
                pltpu.VMEM((rows + half, width), BF16),
                pltpu.VMEM((rows + half, width), BF16),
                pltpu.VMEM((width, key_width), BF16),
                pltpu.VMEM((slots, mol_rows, width), BF16),
                pltpu.VMEM((mol_rows, key_width), BF16),
                pltpu.VMEM((2, half, 2 * half), F32),
                pltpu.VMEM((mol_rows, width), F32),
                pltpu.VMEM((mol_rows, width), BF16),
                pltpu.VMEM((mol_rows, width), BF16),
                pltpu.VMEM((mol_rows, width), BF16),
                pltpu.VMEM((mol_rows, key_width), F32),
                pltpu.VMEM((nown, 1, part), F32),
                pltpu.VMEM((nown, 1, part), F32),
                pltpu.VMEM((nz, 1, part), F32),
                pltpu.VMEM((nown, 1, part), F32),
                dma((6,)),
                dma((2 * chunks,)),
                dma((2 * chunks,)),
                dma((1,)),
                dma((1,)),
                dma((chunks + 1,)),
                dma((chunks + 1,)),
                dma((nown,)),
                dma((nown,)),
                dma((nz,)),
                dma((nz,)),
                dma((nown,)),
                dma((nown,)),
            ],
            compiler_params=pltpu.CompilerParams(
                collective_id=0, has_side_effects=True, vmem_limit_bytes=56 * 1024 * 1024
            ),
        )(q, k, v, doc_starts, w, gain, stashed, cotangent, plan_slot)

    in_specs = (
        P("rep", "section", "seq", None),
        P("rep", "section", "seq", None),
        P("rep", "section", "seq", None),
        P("rep", "section", None),
        P("section", None, None),
        P("section", None),
        P("rep", "section", None, "seq", None),
        P("rep", "section", "seq", None),
        P("rep", "section"),
    )
    out_specs = (
        P("rep", "section", "seq", None),
        P("rep", "section", "seq", None),
        P("section", None),
    )
    return jax.shard_map(local, mesh=mesh, in_specs=in_specs, out_specs=out_specs, check_vma=False)
```

time: 312 us -> 53 us (0.17)
  the two profiles are of different devices: /device:TPU:266 before, /device:TPU:1 now
where the time goes in v1:
time: 53 us; the launch traced here: 52.7 us
  Pallas kernels  46.9 us (88%)
  local copies, waits for them, and re-layouts  4.53 us (9%)
  between operations  1.29 us (2%)
    pallas_call x1, Pallas kernels, local(): pl.pallas_call(functools.partial(kernel, nsec, nseq, nrep, chunks), out_s...  46.9 us
    unnamed x3, local copies, waits for them, and re-layouts  4.53 us

profile of v1, /device:TPU:1, one launch (start us, length us, event | category | flops | bytes accessed | tf_op | source)
XLA Modules:
  0.0 52.7 jit_solution(8851818891618701760)
XLA Ops:
  1.3 46.9 %shard_map.112 = (bf16[1,1,64,1024]{3,2,1,0:T(8,128)(2,1)}, bf16[1,1,64,2048]{3,2,1,0:T(8,128)(2,1)}, f32[1,2048]{1,0:T(1,128)}) custom-call(bf16[1,1,256,2048]{3,2,1,0:T(8,128)(2,1)} %q_hbm.1, bf16[1,1,256,2048]{3,2,1,0:T(8,128)(2,1)} %k_hbm.1, bf16[1,1,256,2048]{3,2,1,0:T(8,128)(2,1)} %v_hbm.1, s32[1,1,48]{2,1,0:T(1,128)} %doc_ref.1, ...), custom_call_target="tpu_custom_call" | custom-call | tf_op jit(solution)/shard_map/pallas_call | solution.py:343
  48.2 1.6 %copy.16 = bf16[1,1,64,1024]{3,2,1,0:T(8,128)(2,1)} copy(bf16[1,1,64,1024]{3,2,1,0:T(8,128)(2,1)} %get-tuple-element.6) | data formatting | bytes 262144
  49.8 1.7 %copy.17 = bf16[1,1,64,2048]{3,2,1,0:T(8,128)(2,1)} copy(bf16[1,1,64,2048]{3,2,1,0:T(8,128)(2,1)} %get-tuple-element.7) | data formatting | bytes 524288
  51.4 1.3 %copy.18 = f32[1,2048]{1,0:T(1,128)} copy(f32[1,2048]{1,0:T(1,128)} %get-tuple-element.8) | data formatting | bytes 16384

commit v2 on v1

v2 whole, which is shorter than its diff:
```python
import functools
import math

import jax
import jax.numpy as jnp
from jax import lax
from jax.experimental import pallas as pl
from jax.experimental.pallas import tpu as pltpu
from jax.sharding import PartitionSpec as P

HEAD_DIM = 64
POOL = 4
WINDOW = 128
EPS_NORM = 1e-05
EPS_STEP = 1e-06
LOG2E = math.log2(math.e)
MESH = pl.DeviceIdType.MESH
F32 = jnp.float32
BF16 = jnp.bfloat16
IN_SPACE = pltpu.HBM
OUT_SHAPE = pltpu.VMEM


def kernel(
    nsec,
    nseq,
    nrep,
    chunks,
    q_hbm,
    k_hbm,
    v_hbm,
    doc_hbm,
    w_hbm,
    gain_hbm,
    st_hbm,
    cot_hbm,
    slot_hbm,
    mol_ref,
    up_ref,
    gu_ref,
    q_raw,
    q_buf,
    k_buf,
    v_buf,
    w_buf,
    st_buf,
    cot_buf,
    doc_ref,
    gain_ref,
    slot_ref,
    bias,
    bg_buf,
    din,
    pooled,
    arrived,
    acc,
    g_own,
    r1,
    r2,
    r3,
    loc_sem,
    ready,
    kv_send,
    kv_recv,
    up_send,
    up_recv,
    po_send,
    po_recv,
    p1_send,
    p1_recv,
    p2_send,
    p2_recv,
    p3_send,
    p3_recv,
):
    rows, width = q_raw.shape
    half = rows // 2
    mol_rows, key_width = acc.shape
    mol_half = mol_rows // 2
    nz = nseq // 2
    nown = nrep * 2
    part = width // nown
    cw = width // chunks
    pairs = cw // 128

    sec = lax.axis_index("section")
    seq = lax.axis_index("seq")
    rep = lax.axis_index("rep")
    core = lax.rem(seq, 2)
    z = lax.div(seq, 2)
    me = rep * 2 + core
    sec_next = lax.rem(sec + 1, nsec)
    sec_prev = lax.rem(sec + nsec - 1, nsec)
    seq_next = lax.rem(seq + 1, nseq)
    across = lax.rem(seq + nseq + 2 * core - 1, nseq)

    def owner_id(d):
        other = lax.rem(me + d, nown)
        return other, {"seq": z * 2 + lax.rem(other, 2), "rep": lax.div(other, 2)}

    def z_id(d):
        other = lax.rem(z + d, nz)
        return other, {"seq": other * 2 + core}

    def signal(sem, peers):
        for peer in peers:
            pl.semaphore_signal(sem, inc=1, device_id=peer, device_id_type=MESH)

    near_z = sorted({d % nz for d in (1, 2, -1, -2)} - {0})
    step_z = sorted({2 % nz, -2 % nz} - {0})
    near = [{"seq": across}, {"section": sec_next}, {"section": sec_prev}]
    near += [owner_id(d)[1] for d in range(1, nown)]
    near += [z_id(d)[1] for d in near_z]
    barrier = pltpu.get_barrier_semaphore()
    signal(barrier, near)

    loads = {}

    def load(name, src, dst):
        loads[name] = pltpu.make_async_copy(src, dst, loc_sem.at[len(loads)])
        loads[name].start()

    load("slot", slot_hbm, slot_ref)
    load("st", st_hbm.at[0, 0], st_buf)
    load("cot", cot_hbm.at[0, 0], cot_buf)
    load("gain", gain_hbm, gain_ref)
    for c in range(chunks):
        load("w%d" % c, w_hbm.at[0, pl.ds(c * cw, cw)], w_buf.at[pl.ds(c * cw, cw)])
    load("doc", doc_hbm.at[0], doc_ref)

    pl.semaphore_wait(barrier, len(near))
    signal(ready.at[0], [z_id(d)[1] for d in step_z])

    def remote(src, dst, send, recv, to):
        return pltpu.make_async_remote_copy(
            src_ref=src, dst_ref=dst, send_sem=send, recv_sem=recv, device_id=to, device_id_type=MESH
        )

    halo = []

    def send_halo(c):
        cols = pl.ds(c * cw, cw)
        for i, (src, dst) in enumerate(((k_hbm, k_buf), (v_hbm, v_buf))):
            copy = remote(
                src.at[0, 0, pl.ds(half, half), cols],
                dst.at[pl.ds(0, half), cols],
                kv_send.at[2 * c + i],
                kv_recv.at[2 * c + i],
                {"seq": seq_next},
            )
            copy.start()
            halo.append(copy)

    for c in range(chunks // 2):
        send_halo(c)

    for name in ("slot", "st"):
        loads[name].wait()
    slot = slot_ref[0, 0]
    square = jnp.zeros((mol_rows, 1), F32)
    for c in range(chunks):
        cols = pl.ds(c * cw, cw)
        held = st_buf[slot, :, cols].astype(F32)
        square += jnp.sum(held * held, axis=1, keepdims=True)
    inv_rms = lax.rsqrt(square / width + EPS_NORM)
    for name in ("cot", "gain"):
        loads[name].wait()
    cot = cot_buf[...]
    mixed = jnp.zeros((mol_rows, 1), F32)
    for c in range(chunks):
        cols = pl.ds(c * cw, cw)
        loads["w%d" % c].wait()
        back = lax.dot_general(cot, w_buf[cols, :], (((1,), (1,)), ((), ())), preferred_element_type=F32)
        whitened = st_buf[slot, :, cols].astype(F32) * inv_rms
        total = jnp.sum(back * whitened, axis=0, keepdims=True)
        for i in range(cw // part):
            g_own[c * (cw // part) + i] = total[:, i * part : (i + 1) * part]
        scaled = back * gain_ref[:, cols]
        bg_buf[:, cols] = scaled
        mixed += jnp.sum(scaled * whitened, axis=1, keepdims=True)

    phase1 = []
    for d in range(1, nown):
        other, to = owner_id(d)
        copy = remote(g_own.at[other], r1.at[d], p1_send.at[d], p1_recv.at[d], to)
        copy.start()
        phase1.append(copy)
    load("q", q_hbm.at[0, 0], q_raw)
    load("k", k_hbm.at[0, 0], k_buf.at[pl.ds(half, rows)])
    load("v", v_hbm.at[0, 0], v_buf.at[pl.ds(half, rows)])

    mixed = mixed / width
    for c in range(chunks):
        cols = pl.ds(c * cw, cw)
        whitened = st_buf[slot, :, cols].astype(F32) * inv_rms
        din[:, cols] = (inv_rms * (bg_buf[:, cols] - whitened * mixed)).astype(BF16)
    if step_z:
        pl.semaphore_wait(ready.at[0], len(step_z))
        signal(ready.at[1], [z_id(d)[1] for d in step_z])
    up_copy = remote(din, up_ref.at[0, 0], up_send.at[0], up_recv.at[0], {"section": sec_prev})
    up_copy.start()

    loads["doc"].wait()
    offsets = doc_ref[...].astype(F32)
    q_row = lax.broadcasted_iota(jnp.int32, (half, 1), 0)
    q_in = POOL * lax.rem(q_row, mol_half) + lax.div(q_row, mol_half)
    k_in = lax.broadcasted_iota(jnp.int32, (half, 2 * half), 1)
    for b in range(2):
        start = seq * rows + b * half
        q_pos = (q_in + start).astype(F32)
        begin = jnp.max(jnp.where(offsets <= q_pos, offsets, -1.0), axis=1, keepdims=True)
        allowed = (
            (k_in > q_in + (half - WINDOW)) & (k_in <= q_in + half) & ((k_in + (start - half)).astype(F32) >= begin)
        )
        bias[b] = jnp.where(allowed, F32(0.0), F32(-1e30))

    row = lax.broadcasted_iota(jnp.int32, (rows, rows), 0)
    col = lax.broadcasted_iota(jnp.int32, (rows, rows), 1)
    inner = lax.rem(row, half)
    source = (row - inner) + POOL * lax.rem(inner, mol_half) + lax.div(inner, mol_half)
    perm = jnp.where(col == source, F32(1.0 / math.sqrt(HEAD_DIM)), F32(0.0)).astype(BF16)
    lane = lax.broadcasted_iota(jnp.int32, (rows, 128), 1)
    loads["q"].wait()
    for c in range(chunks):
        moved = jnp.dot(perm, q_raw[:, pl.ds(c * cw, cw)], preferred_element_type=F32)
        for i in range(pairs):
            cols = pl.ds(c * cw + i * 128, 128)
            piece = moved[:, i * 128 : (i + 1) * 128]
            first = jnp.where(lane < HEAD_DIM, piece, 0.0).astype(BF16)
            second = jnp.where(lane < HEAD_DIM, 0.0, piece).astype(BF16)
            for b in range(2):
                q_buf[b, pl.ds(0, half), cols] = first[b * half : (b + 1) * half]
                q_buf[b, pl.ds(half, half), cols] = second[b * half : (b + 1) * half]

    low = lax.broadcasted_iota(jnp.int32, (half, 128), 1) < HEAD_DIM
    fours = jnp.full((2 * half, 128), POOL, BF16)

    def one_pair(b, pair):
        cols = pl.ds(pl.multiple_of(pair * 128, 128), 128)
        keys = k_buf[pl.ds(b * half, 2 * half), cols]
        values = v_buf[pl.ds(b * half, 2 * half), cols]
        scores = lax.dot_general(q_buf[b, :, cols], keys, (((1,), (1,)), ((), ())), preferred_element_type=F32)
        blocked = bias[b]
        weights = []
        for h in range(2):
            s = scores[h * half : (h + 1) * half] + blocked
            top = jnp.max(s, axis=1, keepdims=True)
            weights.append(jnp.exp2((s - top) * LOG2E).astype(BF16))
        mixed_heads = jnp.dot(
            jnp.concatenate(weights, axis=0),
            jnp.concatenate([values, fours], axis=1),
            preferred_element_type=F32,
        )
        first, second = mixed_heads[:half], mixed_heads[half:]
        out = jnp.where(low, first[:, :128], second[:, :128]) / jnp.where(low, first[:, 128:], second[:, 128:])
        mean = out[:mol_half]
        for t in range(1, POOL):
            mean += out[t * mol_half : (t + 1) * mol_half]
        pooled[pl.ds(b * mol_half, mol_half), cols] = mean.astype(BF16)

    def attend(b, first_pair, count):
        def two_pairs(i, carry):
            one_pair(b, first_pair + 2 * i)
            one_pair(b, first_pair + 2 * i + 1)
            return carry

        lax.fori_loop(0, count // 2, two_pairs, 0)

    relay = []

    def send_pooled(rows_at, cols):
        copy = remote(
            pooled.at[rows_at, cols],
            arrived.at[rows_at, cols],
            po_send.at[len(relay)],
            po_recv.at[len(relay)],
            {"section": sec_next},
        )
        copy.start()
        relay.append(copy)

    all_pairs = width // 128
    loads["k"].wait()
    loads["v"].wait()
    attend(1, 0, all_pairs // 2)

    for copy in phase1:
        copy.wait_recv()
    summed = g_own[me]
    for d in range(1, nown):
        summed += r1[d]
    r2[z] = summed
    if step_z:
        pl.semaphore_wait(ready.at[1], len(step_z))
    phase2 = []
    for d in range(1, nz):
        other, to = z_id(d)
        copy = remote(r2.at[z], r2.at[z], p2_send.at[d], p2_recv.at[d], to)
        copy.start()
        phase2.append(copy)
    for c in range(chunks // 2, chunks):
        send_halo(c)

    attend(1, all_pairs // 2, all_pairs // 2)
    send_pooled(pl.ds(mol_half, mol_half), pl.ds(0, width))
    acc[...] = jnp.zeros_like(acc)
    square = jnp.zeros((mol_rows, 1), F32)

    def near_part(c):
        halo[2 * c].wait_recv()
        halo[2 * c + 1].wait_recv()
        attend(0, c * pairs, pairs)
        send_pooled(pl.ds(0, mol_half), pl.ds(c * cw, cw))

    def project(c, square):
        cols = pl.ds(c * cw, cw)
        relay[1 + c].wait_recv()
        got = arrived[:, cols].astype(F32)
        acc[...] += jnp.dot((got * gain_ref[:, cols]).astype(BF16), w_buf[cols, :], preferred_element_type=F32)
        return square + jnp.sum(got * got, axis=1, keepdims=True)

    for c in range(chunks // 2):
        near_part(c)

    for d in range(1, nz):
        other = lax.rem(z + nz - d, nz)
        remote(r2.at[z], r2.at[other], p2_send.at[d], p2_recv.at[d], {"seq": seq_next}).wait_recv()
    summed = r2[0]
    for i in range(1, nz):
        summed += r2[i]
    r3[me] = summed
    phase3 = []
    for d in range(1, nown):
        other, to = owner_id(d)
        copy = remote(r3.at[me], r3.at[me], p3_send.at[d], p3_recv.at[d], to)
        copy.start()
        phase3.append(copy)

    relay[0].wait_recv()
    for c in range(chunks // 2, chunks):
        near_part(c)
        square = project(c - chunks // 2, square)
    for c in range(chunks - chunks // 2, chunks - 1):
        square = project(c, square)

    for d in range(1, nown):
        other = lax.rem(me + nown - d, nown)
        remote(r3.at[me], r3.at[other], p3_send.at[d], p3_recv.at[d], {"seq": seq_next}).wait_recv()
    power = jnp.zeros((1, 1), F32)
    for i in range(nown):
        power += jnp.sum(r3[i] * r3[i], axis=1, keepdims=True)
    inv_step = 1.0 / jnp.sqrt(power / width + EPS_STEP)
    for i in range(nown):
        gu_ref[:, pl.ds(i * part, part)] = r3[i] * inv_step

    square = project(chunks - 1, square)
    mol_ref[0, 0] = (acc[...] * lax.rsqrt(square / width + EPS_NORM)).astype(BF16)
    for copy in (*halo, *phase1, *phase2, *phase3, *relay):
        copy.wait_send()
    up_copy.wait()


def write_out(*refs):
    count = (len(refs) - 1) // 2
    sem = refs[-1]
    copies = [pltpu.make_async_copy(refs[i], refs[count + i], sem.at[i]) for i in range(count)]
    for copy in copies:
        copy.start()
    for copy in copies:
        copy.wait()


def solution(mesh):
    nsec, nseq, nrep = (mesh.shape[a] for a in ("section", "seq", "rep"))

    def local(q, k, v, doc_starts, w, gain, stashed, cotangent, plan_slot):
        rows, width = q.shape[2:]
        key_width = w.shape[2]
        slots, mol_rows = stashed.shape[2:4]
        half = rows // 2
        chunks = 4 if width >= 2048 else 2
        nz, nown = nseq // 2, nrep * 2
        part = width // nown
        hbm = pl.BlockSpec(memory_space=IN_SPACE)
        vmem = pl.BlockSpec(memory_space=pltpu.VMEM)
        dma = pltpu.SemaphoreType.DMA
        shapes = (
            ((1, 1, mol_rows, key_width), BF16),
            ((1, 1, mol_rows, width), BF16),
            ((1, width), F32),
        )
        results = pl.pallas_call(
            functools.partial(kernel, nsec, nseq, nrep, chunks),
            out_shape=tuple(OUT_SHAPE(s, t) for s, t in shapes),
            in_specs=[hbm] * 9,
            out_specs=(vmem, vmem, vmem),
            scratch_shapes=[
                pltpu.VMEM((rows, width), BF16),
                pltpu.VMEM((2, rows, width), BF16),
                pltpu.VMEM((rows + half, width), BF16),
                pltpu.VMEM((rows + half, width), BF16),
                pltpu.VMEM((width, key_width), BF16),
                pltpu.VMEM((slots, mol_rows, width), BF16),
                pltpu.VMEM((mol_rows, key_width), BF16),
                pltpu.VMEM((1, doc_starts.shape[2]), jnp.int32),
                pltpu.VMEM((1, width), F32),
                pltpu.SMEM((1, 1), jnp.int32),
                pltpu.VMEM((2, half, 2 * half), F32),
                pltpu.VMEM((mol_rows, width), F32),
                pltpu.VMEM((mol_rows, width), BF16),
                pltpu.VMEM((mol_rows, width), BF16),
                pltpu.VMEM((mol_rows, width), BF16),
                pltpu.VMEM((mol_rows, key_width), F32),
                pltpu.VMEM((nown, 1, part), F32),
                pltpu.VMEM((nown, 1, part), F32),
                pltpu.VMEM((nz, 1, part), F32),
                pltpu.VMEM((nown, 1, part), F32),
                dma((8 + chunks,)),
                pltpu.SemaphoreType.REGULAR((2,)),
                dma((2 * chunks,)),
                dma((2 * chunks,)),
                dma((1,)),
                dma((1,)),
                dma((chunks + 1,)),
                dma((chunks + 1,)),
                dma((nown,)),
                dma((nown,)),
                dma((nz,)),
                dma((nz,)),
                dma((nown,)),
                dma((nown,)),
            ],
            compiler_params=pltpu.CompilerParams(
                collective_id=0, has_side_effects=True, vmem_limit_bytes=56 * 1024 * 1024
            ),
        )(q, k, v, doc_starts, w, gain, stashed, cotangent, plan_slot)
        any_space = pl.BlockSpec(memory_space=pl.ANY)
        return pl.pallas_call(
            write_out,
            out_shape=tuple(jax.ShapeDtypeStruct(s, t) for s, t in shapes),
            in_specs=[vmem] * 3,
            out_specs=(any_space,) * 3,
            scratch_shapes=[dma((3,))],
        )(*(pltpu.with_memory_space_constraint(r, pltpu.VMEM) for r in results))

    in_specs = (
        P("rep", "section", "seq", None),
        P("rep", "section", "seq", None),
        P("rep", "section", "seq", None),
        P("rep", "section", None),
        P("section", None, None),
        P("section", None),
        P("rep", "section", None, "seq", None),
        P("rep", "section", "seq", None),
        P("rep", "section"),
    )
    out_specs = (
        P("rep", "section", "seq", None),
        P("rep", "section", "seq", None),
        P("section", None),
    )
    return jax.shard_map(local, mesh=mesh, in_specs=in_specs, out_specs=out_specs, check_vma=False)
```

time: 53 us -> 40.7 us (0.77)
  Pallas kernels: 46.9 us -> 39.2 us
  local copies, waits for them, and re-layouts: 4.53 us -> 0 us
    pallas_call x1, Pallas kernels: 46.9 us -> 38.4 us  [local(): pl.pallas_call(functools.partial(kernel, nsec, nseq, nrep, chunks), out_s...]
    unnamed x3 -> x0, local copies, waits for them, and re-layouts: 4.53 us -> none
    pallas_call x0 -> x1, Pallas kernels: none -> 0.78 us  [local(): pl.pallas_call(write_out, out_shape=tuple((jax.ShapeDtypeStruct(s, t) for...]
where the time goes in v2:
time: 40.7 us; the launch traced here: 40.5 us
  Pallas kernels  39.2 us (96%)
  between operations  1.29 us (3%)
    pallas_call x1, Pallas kernels, local(): pl.pallas_call(functools.partial(kernel, nsec, nseq, nrep, chunks), out_s...  38.4 us

profile of v2, /device:TPU:1, one launch (start us, length us, event | category | flops | bytes accessed | tf_op | source)
XLA Modules:
  0.0 40.5 jit_solution(17252999967330479440)
XLA Ops:
  1.3 38.4 %shard_map.112 = (bf16[1,1,64,1024]{3,2,1,0:T(8,128)(2,1)S(1)}, bf16[1,1,64,2048]{3,2,1,0:T(8,128)(2,1)S(1)}, f32[1,2048]{1,0:T(1,128)S(1)}) custom-call(bf16[1,1,256,2048]{3,2,1,0:T(8,128)(2,1)} %q_hbm.1, bf16[1,1,256,2048]{3,2,1,0:T(8,128)(2,1)} %k_hbm.1, bf16[1,1,256,2048]{3,2,1,0:T(8,128)(2,1)} %v_hbm.1, s32[1,1,48]{2,1,0:T(1,128)} %doc_hbm.1, ...), custom_call_target="tpu_custom_call" | custom-call | tf_op jit(solution)/shard_map/pallas_call | solution.py:392
  39.7 0.8 %shard_map.113 = (bf16[1,1,64,1024]{3,2,1,0:T(8,128)(2,1)}, bf16[1,1,64,2048]{3,2,1,0:T(8,128)(2,1)}, f32[1,2048]{1,0:T(1,128)}) custom-call(bf16[1,1,64,1024]{3,2,1,0:T(8,128)(2,1)S(1)} %get-tuple-element.6.refs_0_, bf16[1,1,64,2048]{3,2,1,0:T(8,128)(2,1)S(1)} %get-tuple-element.7.refs_1_, f32[1,2048]{1,0:T(1,128)S(1)} %get-tuple-element.8.refs_2_), custom_call_target="tpu_custom_call" | custom-call | tf_op jit(solution)/shard_map/pallas_call | solution.py:438

commit v3 on v2

--- a/solution.py
+++ b/solution.py
@@ -13,6 +13,10 @@
 WINDOW = 128
 EPS_NORM = 1e-05
 EPS_STEP = 1e-06
+EARLY = 3
+BEFORE = 3
+CHUNKS = 4
+UNROLL = 4
 LOG2E = math.log2(math.e)
 MESH = pl.DeviceIdType.MESH
 F32 = jnp.float32
@@ -54,6 +58,7 @@
     pooled,
     arrived,
     acc,
+    perm,
     g_own,
     r1,
     r2,
@@ -109,7 +114,11 @@
     near_z = sorted({d % nz for d in (1, 2, -1, -2)} - {0})
     step_z = sorted({2 % nz, -2 % nz} - {0})
     near = [{"seq": across}, {"section": sec_next}, {"section": sec_prev}]
-    near += [owner_id(d)[1] for d in range(1, nown)]
+    step_rep = sorted({1 % nrep, -1 % nrep} - {0})
+    for d in [0] + step_rep:
+        for e in range(2):
+            if d or e:
+                near.append({"seq": z * 2 + lax.rem(core + e, 2), "rep": lax.rem(rep + d, nrep)})
     near += [z_id(d)[1] for d in near_z]
     barrier = pltpu.get_barrier_semaphore()
     signal(barrier, near)
@@ -120,16 +129,45 @@
         loads[name] = pltpu.make_async_copy(src, dst, loc_sem.at[len(loads)])
         loads[name].start()
 
+    load("doc", doc_hbm.at[0], doc_ref)
     load("slot", slot_hbm, slot_ref)
     load("st", st_hbm.at[0, 0], st_buf)
     load("cot", cot_hbm.at[0, 0], cot_buf)
     load("gain", gain_hbm, gain_ref)
     for c in range(chunks):
         load("w%d" % c, w_hbm.at[0, pl.ds(c * cw, cw)], w_buf.at[pl.ds(c * cw, cw)])
-    load("doc", doc_hbm.at[0], doc_ref)
-
+
+    loads["doc"].wait()
+    offsets = doc_ref[...].astype(F32)
+    q_row = lax.broadcasted_iota(jnp.int32, (half, 1), 0)
+    shift = mol_half.bit_length() - 1
+    q_in = POOL * (q_row & (mol_half - 1)) + (q_row >> shift)
+    k_in = lax.broadcasted_iota(jnp.int32, (half, 2 * half), 1)
+    for b in range(2):
+        start = seq * rows + b * half
+        q_pos = (q_in + start).astype(F32)
+        begin = jnp.max(jnp.where(offsets <= q_pos, offsets, -1.0), axis=1, keepdims=True)
+        least = jnp.maximum(q_in + (half - WINDOW + 1), begin.astype(jnp.int32) + half - start)
+        bias[b] = jnp.where((k_in >= least) & (k_in <= q_in + half), F32(0.0), F32(-1e30))
+
+    row = lax.broadcasted_iota(jnp.int32, (rows, 1), 0)
+    inner = row & (half - 1)
+    source = (row - inner) + POOL * (inner & (mol_half - 1)) + (inner >> shift)
+    col = lax.broadcasted_iota(jnp.int32, (rows, rows), 1)
+    perm[...] = jnp.where(col == source, F32(1.0 / math.sqrt(HEAD_DIM)), F32(0.0)).astype(BF16)
+
+    for name in ("slot", "st"):
+        loads[name].wait()
+    slot = slot_ref[0, 0]
+    square = jnp.zeros((mol_rows, 1), F32)
+    for c in range(chunks):
+        cols = pl.ds(c * cw, cw)
+        held = st_buf[slot, :, cols].astype(F32)
+        square += jnp.sum(held * held, axis=1, keepdims=True)
+    inv_rms = lax.rsqrt(square / width + EPS_NORM)
     pl.semaphore_wait(barrier, len(near))
-    signal(ready.at[0], [z_id(d)[1] for d in step_z])
+    onward = [z_id(d)[1] for d in step_z] + [{"rep": lax.rem(rep + d, nrep)} for d in step_rep]
+    signal(ready.at[0], onward)
 
     def remote(src, dst, send, recv, to):
         return pltpu.make_async_remote_copy(
@@ -151,18 +189,10 @@
             copy.start()
             halo.append(copy)
 
-    for c in range(chunks // 2):
+    early = min(EARLY, chunks - 1)
+    for c in range(early):
         send_halo(c)
 
-    for name in ("slot", "st"):
-        loads[name].wait()
-    slot = slot_ref[0, 0]
-    square = jnp.zeros((mol_rows, 1), F32)
-    for c in range(chunks):
-        cols = pl.ds(c * cw, cw)
-        held = st_buf[slot, :, cols].astype(F32)
-        square += jnp.sum(held * held, axis=1, keepdims=True)
-    inv_rms = lax.rsqrt(square / width + EPS_NORM)
     for name in ("cot", "gain"):
         loads[name].wait()
     cot = cot_buf[...]
@@ -179,6 +209,10 @@
         bg_buf[:, cols] = scaled
         mixed += jnp.sum(scaled * whitened, axis=1, keepdims=True)
 
+    if onward:
+        pl.semaphore_wait(ready.at[0], len(onward))
+    signal(ready.at[1], [z_id(d)[1] for d in step_z])
+
     phase1 = []
     for d in range(1, nown):
         other, to = owner_id(d)
@@ -194,35 +228,13 @@
         cols = pl.ds(c * cw, cw)
         whitened = st_buf[slot, :, cols].astype(F32) * inv_rms
         din[:, cols] = (inv_rms * (bg_buf[:, cols] - whitened * mixed)).astype(BF16)
-    if step_z:
-        pl.semaphore_wait(ready.at[0], len(step_z))
-        signal(ready.at[1], [z_id(d)[1] for d in step_z])
     up_copy = remote(din, up_ref.at[0, 0], up_send.at[0], up_recv.at[0], {"section": sec_prev})
     up_copy.start()
 
-    loads["doc"].wait()
-    offsets = doc_ref[...].astype(F32)
-    q_row = lax.broadcasted_iota(jnp.int32, (half, 1), 0)
-    q_in = POOL * lax.rem(q_row, mol_half) + lax.div(q_row, mol_half)
-    k_in = lax.broadcasted_iota(jnp.int32, (half, 2 * half), 1)
-    for b in range(2):
-        start = seq * rows + b * half
-        q_pos = (q_in + start).astype(F32)
-        begin = jnp.max(jnp.where(offsets <= q_pos, offsets, -1.0), axis=1, keepdims=True)
-        allowed = (
-            (k_in > q_in + (half - WINDOW)) & (k_in <= q_in + half) & ((k_in + (start - half)).astype(F32) >= begin)
-        )
-        bias[b] = jnp.where(allowed, F32(0.0), F32(-1e30))
-
-    row = lax.broadcasted_iota(jnp.int32, (rows, rows), 0)
-    col = lax.broadcasted_iota(jnp.int32, (rows, rows), 1)
-    inner = lax.rem(row, half)
-    source = (row - inner) + POOL * lax.rem(inner, mol_half) + lax.div(inner, mol_half)
-    perm = jnp.where(col == source, F32(1.0 / math.sqrt(HEAD_DIM)), F32(0.0)).astype(BF16)
     lane = lax.broadcasted_iota(jnp.int32, (rows, 128), 1)
     loads["q"].wait()
     for c in range(chunks):
-        moved = jnp.dot(perm, q_raw[:, pl.ds(c * cw, cw)], preferred_element_type=F32)
+        moved = jnp.dot(perm[...], q_raw[:, pl.ds(c * cw, cw)], preferred_element_type=F32)
         for i in range(pairs):
             cols = pl.ds(c * cw + i * 128, 128)
             piece = moved[:, i * 128 : (i + 1) * 128]
@@ -259,12 +271,14 @@
         pooled[pl.ds(b * mol_half, mol_half), cols] = mean.astype(BF16)
 
     def attend(b, first_pair, count):
-        def two_pairs(i, carry):
-            one_pair(b, first_pair + 2 * i)
-            one_pair(b, first_pair + 2 * i + 1)
+        unroll = min(UNROLL, count)
+
+        def few_pairs(i, carry):
+            for j in range(unroll):
+                one_pair(b, first_pair + unroll * i + j)
             return carry
 
-        lax.fori_loop(0, count // 2, two_pairs, 0)
+        lax.fori_loop(0, count // unroll, few_pairs, 0)
 
     relay = []
 
@@ -298,7 +312,7 @@
         copy = remote(r2.at[z], r2.at[z], p2_send.at[d], p2_recv.at[d], to)
         copy.start()
         phase2.append(copy)
-    for c in range(chunks // 2, chunks):
+    for c in range(early, chunks):
         send_halo(c)
 
     attend(1, all_pairs // 2, all_pairs // 2)
@@ -319,7 +333,8 @@
         acc[...] += jnp.dot((got * gain_ref[:, cols]).astype(BF16), w_buf[cols, :], preferred_element_type=F32)
         return square + jnp.sum(got * got, axis=1, keepdims=True)
 
-    for c in range(chunks // 2):
+    before = min(BEFORE, chunks - 1)
+    for c in range(before):
         near_part(c)
 
     for d in range(1, nz):
@@ -337,11 +352,15 @@
         phase3.append(copy)
 
     relay[0].wait_recv()
-    for c in range(chunks // 2, chunks):
+    done = 0
+    for c in range(before, chunks):
         near_part(c)
-        square = project(c - chunks // 2, square)
-    for c in range(chunks - chunks // 2, chunks - 1):
-        square = project(c, square)
+        if done < c:
+            square = project(done, square)
+            done += 1
+    while done < chunks - 1:
+        square = project(done, square)
+        done += 1
 
     for d in range(1, nown):
         other = lax.rem(me + nown - d, nown)
@@ -378,7 +397,7 @@
         key_width = w.shape[2]
         slots, mol_rows = stashed.shape[2:4]
         half = rows // 2
-        chunks = 4 if width >= 2048 else 2
+        chunks = CHUNKS if width >= 2048 else 2
         nz, nown = nseq // 2, nrep * 2
         part = width // nown
         hbm = pl.BlockSpec(memory_space=IN_SPACE)
@@ -411,6 +430,7 @@
                 pltpu.VMEM((mol_rows, width), BF16),
                 pltpu.VMEM((mol_rows, width), BF16),
                 pltpu.VMEM((mol_rows, key_width), F32),
+                pltpu.VMEM((rows, rows), BF16),
                 pltpu.VMEM((nown, 1, part), F32),
                 pltpu.VMEM((nown, 1, part), F32),
                 pltpu.VMEM((nz, 1, part), F32),

time: 40.7 us -> 39 us (0.958)
  Pallas kernels: 39.2 us -> 37.2 us
    pallas_call x1, Pallas kernels: 38.4 us -> 36.4 us  [local(): pl.pallas_call(functools.partial(kernel, nsec, nseq, nrep, chunks), out_s...]
where the time goes in v3:
time: 39 us; the launch traced here: 38.5 us
  Pallas kernels  37.2 us (95%)
  between operations  1.29 us (3%)
    pallas_call x1, Pallas kernels, local(): pl.pallas_call(functools.partial(kernel, nsec, nseq, nrep, chunks), out_s...  36.4 us

profile of v3, /device:TPU:1, one launch (start us, length us, event | category | flops | bytes accessed | tf_op | source)
XLA Modules:
  0.0 38.5 jit_solution(13186512492628646212)
XLA Ops:
  1.3 36.4 %shard_map.112 = (bf16[1,1,64,1024]{3,2,1,0:T(8,128)(2,1)S(1)}, bf16[1,1,64,2048]{3,2,1,0:T(8,128)(2,1)S(1)}, f32[1,2048]{1,0:T(1,128)S(1)}) custom-call(bf16[1,1,256,2048]{3,2,1,0:T(8,128)(2,1)} %q_hbm.1, bf16[1,1,256,2048]{3,2,1,0:T(8,128)(2,1)} %k_hbm.1, bf16[1,1,256,2048]{3,2,1,0:T(8,128)(2,1)} %v_hbm.1, s32[1,1,48]{2,1,0:T(1,128)} %doc_hbm.1, ...), custom_call_target="tpu_custom_call" | custom-call | tf_op jit(solution)/shard_map/pallas_call | solution.py:411
  37.7 0.8 %shard_map.113 = (bf16[1,1,64,1024]{3,2,1,0:T(8,128)(2,1)}, bf16[1,1,64,2048]{3,2,1,0:T(8,128)(2,1)}, f32[1,2048]{1,0:T(1,128)}) custom-call(bf16[1,1,64,1024]{3,2,1,0:T(8,128)(2,1)S(1)} %get-tuple-element.6.refs_0_, bf16[1,1,64,2048]{3,2,1,0:T(8,128)(2,1)S(1)} %get-tuple-element.7.refs_1_, f32[1,2048]{1,0:T(1,128)S(1)} %get-tuple-element.8.refs_2_), custom_call_target="tpu_custom_call" | custom-call | tf_op jit(solution)/shard_map/pallas_call | solution.py:458

commit v4 on v3

--- a/solution.py
+++ b/solution.py
@@ -297,6 +297,7 @@
     loads["k"].wait()
     loads["v"].wait()
     attend(1, 0, all_pairs // 2)
+    send_pooled(pl.ds(mol_half, mol_half), pl.ds(0, width // 2))
 
     for copy in phase1:
         copy.wait_recv()
@@ -316,7 +317,7 @@
         send_halo(c)
 
     attend(1, all_pairs // 2, all_pairs // 2)
-    send_pooled(pl.ds(mol_half, mol_half), pl.ds(0, width))
+    send_pooled(pl.ds(mol_half, mol_half), pl.ds(width // 2, width // 2))
     acc[...] = jnp.zeros_like(acc)
     square = jnp.zeros((mol_rows, 1), F32)
 
@@ -328,7 +329,7 @@
 
     def project(c, square):
         cols = pl.ds(c * cw, cw)
-        relay[1 + c].wait_recv()
+        relay[2 + c].wait_recv()
         got = arrived[:, cols].astype(F32)
         acc[...] += jnp.dot((got * gain_ref[:, cols]).astype(BF16), w_buf[cols, :], preferred_element_type=F32)
         return square + jnp.sum(got * got, axis=1, keepdims=True)
@@ -352,6 +353,7 @@
         phase3.append(copy)
 
     relay[0].wait_recv()
+    relay[1].wait_recv()
     done = 0
     for c in range(before, chunks):
         near_part(c)
@@ -441,8 +443,8 @@
                 dma((2 * chunks,)),
                 dma((1,)),
                 dma((1,)),
-                dma((chunks + 1,)),
-                dma((chunks + 1,)),
+                dma((chunks + 2,)),
+                dma((chunks + 2,)),
                 dma((nown,)),
                 dma((nown,)),
                 dma((nz,)),

time: 39 us -> 39 us (level)
  no operation moved by 1% of the time
where the time goes in v4:
time: 39 us; the launch traced here: 38.5 us
  Pallas kernels  37.2 us (95%)
  between operations  1.29 us (3%)
    pallas_call x1, Pallas kernels, local(): pl.pallas_call(functools.partial(kernel, nsec, nseq, nrep, chunks), out_s...  36.4 us

profile of v4, /device:TPU:1, one launch (start us, length us, event | category | flops | bytes accessed | tf_op | source)
XLA Modules:
  0.0 38.5 jit_solution(10895407149305456669)
XLA Ops:
  1.3 36.4 %shard_map.112 = (bf16[1,1,64,1024]{3,2,1,0:T(8,128)(2,1)S(1)}, bf16[1,1,64,2048]{3,2,1,0:T(8,128)(2,1)S(1)}, f32[1,2048]{1,0:T(1,128)S(1)}) custom-call(bf16[1,1,256,2048]{3,2,1,0:T(8,128)(2,1)} %q_hbm.1, bf16[1,1,256,2048]{3,2,1,0:T(8,128)(2,1)} %k_hbm.1, bf16[1,1,256,2048]{3,2,1,0:T(8,128)(2,1)} %v_hbm.1, s32[1,1,48]{2,1,0:T(1,128)} %doc_hbm.1, ...), custom_call_target="tpu_custom_call" | custom-call | tf_op jit(solution)/shard_map/pallas_call | solution.py:413
  37.7 0.8 %shard_map.113 = (bf16[1,1,64,1024]{3,2,1,0:T(8,128)(2,1)}, bf16[1,1,64,2048]{3,2,1,0:T(8,128)(2,1)}, f32[1,2048]{1,0:T(1,128)}) custom-call(bf16[1,1,64,1024]{3,2,1,0:T(8,128)(2,1)S(1)} %get-tuple-element.6.refs_0_, bf16[1,1,64,2048]{3,2,1,0:T(8,128)(2,1)S(1)} %get-tuple-element.7.refs_1_, f32[1,2048]{1,0:T(1,128)S(1)} %get-tuple-element.8.refs_2_), custom_call_target="tpu_custom_call" | custom-call | tf_op jit(solution)/shard_map/pallas_call | solution.py:460
